TPU v7x, 32 devices: a whole 2x2x4 slice. The times are simulated.
32 devices in a mesh: groups: 2 (over x), expert: 16 (over z, y, core).
Axes of the slice: x: 2, y: 2, z: 4, core: 2. Of those that a mesh axis runs over, the one named last changes fastest.
Arguments:
- hidden_in: bfloat16 [4096, 2048], P(('groups', 'expert')), parts along dimension 0, may hold values from -6 to 6
- norm_gain: float32 [2048], replicated, may hold values from 0.1 to 1.9
- router_weight: bfloat16 [2048, 16], replicated, may hold values from -0.125 to 0.125
- expert_ids: int32 [4096, 8], P(('groups', 'expert')), parts along dimension 0, may hold values from 0 to 15, all different within a row; in each aligned block of 128 rows (0 to 127, 128 to 255, ...) at most 96 rows name the same one
- w_gate: bfloat16 [16, 2048, 768], P('expert'), may hold values from -0.125 to 0.125
- w_up: bfloat16 [16, 2048, 768], P('expert'), may hold values from -0.125 to 0.125
- w_down: bfloat16 [16, 768, 2048], P('expert'), may hold values from -0.21875 to 0.21875
Outputs:
- combined: bfloat16 [4096, 2048], P(('groups', 'expert')), parts along dimension 0
There are 2 independent parts, one for each index of `groups`. A program takes and returns all parts, laid end to end along the dimension named above; an argument that names none is the same for every part. Nothing has to cross between parts.
Inputs may be any that keep to these rules, and one draw needn't show every extreme that they name: `expert_ids`: each row names 8 different experts; within each aligned block of 128 rows (the rows of one device) no expert is named by more than 96 rows, a bound that some block reaches.
All inputs are finite; a program needn't handle non-finite values.
Results may differ from a plain program's by a relative error of at most 0.0074.
Values may be sent and summed in bfloat16 or wider, within the bound.
A program may use at most 128 MiB of HBM per device.

v0:
```python
import jax
import jax.numpy as jnp
from jax import lax
from jax.sharding import PartitionSpec as P


def local(hidden_in, norm_gain, router_weight, expert_ids, w_gate, w_up, w_down):
    tok_rows = hidden_in.shape[0]
    top_count = expert_ids.shape[1]
    num_experts = router_weight.shape[1]
    dev_count = lax.axis_size("expert")
    local_experts = w_gate.shape[0]
    cap_rows = tok_rows * top_count * 3 // (2 * num_experts)
    as_float = hidden_in.astype(jnp.float32)
    inv_rms = lax.rsqrt(jnp.mean(as_float * as_float, axis=1, keepdims=True) + 1e-06)
    normed = (as_float * inv_rms * norm_gain).astype(jnp.bfloat16)
    logits = jnp.dot(normed, router_weight, preferred_element_type=jnp.float32)
    exp_logits = jnp.exp(logits)
    expert_iota = jnp.arange(num_experts, dtype=jnp.int32)
    choice_hot = (expert_ids[:, :, None] == expert_iota[None, None, :]).astype(jnp.float32)
    picked = jnp.sum(choice_hot * exp_logits[:, None, :], axis=2)
    route_w = picked / jnp.sum(picked, axis=1, keepdims=True)
    flat_ids = expert_ids.reshape(-1)
    onehot = (flat_ids[:, None] == expert_iota[None, :]).astype(jnp.int32)
    before = jnp.cumsum(onehot, axis=0) - onehot
    slot_index = jnp.sum(before * onehot, axis=1)
    dest_index = (
        flat_ids // local_experts * cap_rows + slot_index
    ) * local_experts + flat_ids % local_experts
    token_rows = jnp.repeat(normed, top_count, axis=0)
    outgoing = (
        jnp.zeros((num_experts * cap_rows, normed.shape[1]), jnp.bfloat16)
        .at[dest_index]
        .set(token_rows)
    )
    outgoing = outgoing.reshape(dev_count, cap_rows, local_experts, normed.shape[1])
    arrived = lax.all_to_all(outgoing, "expert", split_axis=0, concat_axis=0, tiled=True)
    gate_act = jnp.einsum("smed,edf->smef", arrived, w_gate, preferred_element_type=jnp.float32)
    up_act = jnp.einsum("smed,edf->smef", arrived, w_up, preferred_element_type=jnp.float32)
    hidden = (jax.nn.silu(gate_act) * up_act).astype(jnp.bfloat16)
    returned = lax.all_to_all(
        jnp.einsum("smef,efd->smed", hidden, w_down, preferred_element_type=jnp.float32).astype(
            jnp.bfloat16
        ),
        "expert",
        split_axis=0,
        concat_axis=0,
        tiled=True,
    )
    returned = returned.reshape(num_experts * cap_rows, normed.shape[1])
    gathered = returned[dest_index].reshape(tok_rows, top_count, normed.shape[1])
    combined = jnp.sum(gathered.astype(jnp.float32) * route_w[:, :, None], axis=1).astype(
        jnp.bfloat16
    )
    return combined


def solution(mesh):
    in_specs = (
        P(("groups", "expert"), None),
        P(),
        P(),
        P(("groups", "expert"), None),
        P("expert", None, None),
        P("expert", None, None),
        P("expert", None, None),
    )
    out_specs = P(("groups", "expert"), None)
    return jax.shard_map(local, mesh=mesh, in_specs=in_specs, out_specs=out_specs, check_vma=False)
```

profile of v0, /device:TPU:15, one launch (start us, length us, event | category | flops | bytes accessed | tf_op | source)
XLA Modules:
  0.0 354.0 jit_solution(13436347442580943173)
XLA Ops:
  0.0 0.8 broadcast_multiply_fusion
  0.8 0.9 copy.28
  1.7 0.1 eq.44
  1.8 0.1 eq.40
  1.9 1.2 fusion.29
  3.2 0.1 copy.27
  3.3 0.1 mul.63
  3.4 4.5 %reduce-window.6 = s32[16,8,128]{2,1,0:T(8,128)S(1)} reduce-window(s32[16,8,128]{2,1,0:T(8,128)S(1)} %fusion.35, s32[]{:T(128)} %constant.40.clone.1), window={size=1x1x128 pad=0_0x0_0x127_0}, to_apply=%region_0.0 | reduce-window | flops 2080768 | bytes 131076 | tf_op jit(solution)/shard_map/reduce-window
  7.9 0.1 slice.10
  8.0 0.1 copy.30
  8.2 0.1 copy.31
  8.2 0.1 broadcast_add_fusion
  8.4 2.0 fusion.31
  10.4 10.7 %scatter_custom_fusion = bf16[1536,2048]{1,0:T(8,128)(2,1)} fusion(s32[1024]{0:T(1024)S(1)} %bitcast.108, bf16[]{:T(256)} %constant.38.clone.1, bf16[128,2048]{1,0:T(8,128)(2,1)} %fusion.31), kind=kCustom, calls=%fused_computation.16 | custom fusion | bytes 6815746 | tf_op jit(solution)/shard_map/scatter | solution.py:34
  21.1 144.0 %all_to_all.10 = bf16[16,96,1,2048]{3,1,2,0:T(8,128)(2,1)S(1)} all-to-all(bf16[16,96,1,2048]{3,1,2,0:T(8,128)(2,1)} %bitcast.104), channel_id=1, replica_groups=mesh['groups'=2,'expert'=16] {'expert'}, dimensions={0} | all-to-all | bytes 12582912 | tf_op jit(solution)/shard_map/all_to_all | solution.py:37
  165.1 2.7 copy-done.1
  167.7 6.6 %fusion.1 = f32[16,96,768]{2,1,0:T(8,128)} fusion(bf16[16,96,1,2048]{3,1,2,0:T(8,128)(2,1)S(1)} %all_to_all.10, bf16[1,2048,768]{2,1,0:T(8,128)(2,1)S(1)} %copy-done.4), kind=kOutput, calls=%fused_computation.4 | convolution fusion | flops 4831838208 | bytes 14155776 | tf_op jit(solution)/shard_map/smed,edf->smef/dot_general | solution.py:39
  174.3 16.8 %convert_bitcast_fusion = bf16[16,96,1,2048]{3,1,2,0:T(8,128)(2,1)} fusion(bf16[1,768,2048]{2,1,0:T(8,128)(2,1)S(1)} %copy-done, f32[16,96,768]{2,1,0:T(8,128)} %fusion.1, bf16[1,2048,768]{2,1,0:T(8,128)(2,1)} %param.11, bf16[16,96,1,2048]{3,1,2,0:T(8,128)(2,1)} %copy-done.1), kind=kOutput, calls=%fused_computation.8 | convolution fusion | flops 9673900032 | bytes 23592960 | tf_op jit(solution)/shard_map/smef,efd->smed/dot_general | solution.py:42
  191.2 5.6 %all-to-all-start.1 = ((bf16[16,96,1,2048]{3,1,2,0:T(8,128)(2,1)}), bf16[16,96,1,2048]{3,1,2,0:T(8,128)(2,1)}, u32[]{:S(2)}, u32[]{:S(2)}) async-start(bf16[16,96,1,2048]{3,1,2,0:T(8,128)(2,1)} %convert_bitcast_fusion), calls=%async_computation.1 | async-start | bytes 12582912 | tf_op jit(solution)/shard_map/all_to_all | solution.py:41
  196.8 1.3 convolution_exponential_fusion
  198.2 0.1 copy.33
  198.3 135.9 %all-to-all-done.1 = bf16[16,96,1,2048]{3,1,2,0:T(8,128)(2,1)} async-done(((bf16[16,96,1,2048]{3,1,2,0:T(8,128)(2,1)}), bf16[16,96,1,2048]{3,1,2,0:T(8,128)(2,1)}, u32[]{:S(2)}, u32[]{:S(2)}) %all-to-all-start.1) | async-done | bytes 6291488 | tf_op jit(solution)/shard_map/all_to_all | solution.py:41
  334.2 12.4 %gather_fusion = bf16[1024,2048]{1,0:T(8,128)(2,1)} fusion(bf16[1536,2048]{1,0:T(8,128)(2,1)} %bitcast.26, s32[1024]{0:T(1024)S(1)} %broadcast_clamp_fusion), kind=kCustom, calls=%fused_computation | custom fusion | bytes 8392704 | tf_op jit(solution)/shard_map/gather | solution.py:51
  346.7 7.3 %fusion = bf16[128,2048]{1,0:T(8,128)(2,1)} fusion(bf16[1024,2048]{1,0:T(8,128)(2,1)} %gather_fusion, f32[128,8]{1,0:T(8,128)S(1)} %copy.33), kind=kLoop, calls=%fused_computation.3 | loop fusion | flops 6029312 | bytes 4722688 | tf_op jit(solution)/shard_map/reduce_sum | solution.py:52
  (18 shorter events, 0.2 us)
Async XLA Ops:
  0.0 174.3 %copy-start = (bf16[1,768,2048]{2,1,0:T(8,128)(2,1)S(1)}, bf16[1,768,2048]{2,1,0:T(8,128)(2,1)}, u32[]{:S(2)}) copy-start(bf16[1,768,2048]{2,1,0:T(8,128)(2,1)} %param.13) | copy-start | bytes 9437188
  21.1 146.7 %copy-start.4 = (bf16[1,2048,768]{2,1,0:T(8,128)(2,1)S(1)}, bf16[1,2048,768]{2,1,0:T(8,128)(2,1)}, u32[]{:S(2)}) copy-start(bf16[1,2048,768]{2,1,0:T(8,128)(2,1)} %param.12) | copy-start | bytes 9437188
  165.1 2.7 copy-start.1
  191.2 5.6 %copy-start.2 = (bf16[2048,16]{0,1:T(8,128)(2,1)S(1)}, bf16[2048,16]{0,1:T(8,128)(2,1)}, u32[]{:S(2)}) copy-start(bf16[2048,16]{0,1:T(8,128)(2,1)} %param.9) | copy-start | bytes 196612
  191.2 6.9 %copy-start.3 = (s32[128,8]{0,1:T(8,128)S(1)}, s32[128,8]{0,1:T(8,128)}, u32[]{:S(2)}) copy-start(s32[128,8]{0,1:T(8,128)} %param.10) | copy-start | bytes 12292
  191.2 143.1 %all-to-all-start.1 = ((bf16[16,96,1,2048]{3,1,2,0:T(8,128)(2,1)}), bf16[16,96,1,2048]{3,1,2,0:T(8,128)(2,1)}, u32[]{:S(2)}, u32[]{:S(2)}) async-start(bf16[16,96,1,2048]{3,1,2,0:T(8,128)(2,1)} %convert_bitcast_fusion), calls=%async_computation.1 | async-start | bytes 12582912 | tf_op jit(solution)/shard_map/all_to_all | solution.py:41
where the time goes:
time: 354 us
  blocking collectives  144 us (41%)
  waiting for transfers between devices  136 us (38%)
  local copies, waits for them, and re-layouts  27.4 us (8%)
  matrix products  24.7 us (7%)
  other arithmetic  16.2 us (5%)
  starting transfers between devices  5.64 us (2%)
    all_to_all x1, blocking collectives, local(): lax.all_to_all(outgoing, 'expert', split_axis=0, concat_axis=0, tiled=True)  144 us
    all_to_all x1, waiting for transfers between devices, local(): lax.all_to_all(jnp.einsum('smef,efd->smed', hidden, w_down, preferred_ele...  136 us
    dot_general x1, matrix products, local(): jnp.einsum('smef,efd->smed', hidden, w_down, preferred_element_type=jnp.f...  16.8 us
    gather x1, local copies, waits for them, and re-layouts, local(): returned[dest_index].reshape(tok_rows, top_count, normed.shape[1])  12.4 us
    scatter x1, local copies, waits for them, and re-layouts, local(): outgoing = jnp.zeros((num_experts * cap_rows, normed.shape[1]), jnp.bfloa...  10.7 us
    reduce_sum x1, other arithmetic, local(): jnp.sum(gathered.astype(jnp.float32) * route_w[:, :, None], axis=1)  7.32 us
  transfers between devices with their start and end apart: 1, of which 1 were waited for; matrix products, arithmetic and copies ran while one was open for 0% of the time, Pallas kernels for 0%

commit v1 on v0

--- a/solution.py
+++ b/solution.py
@@ -38,15 +38,18 @@
     gate_act = jnp.einsum("smed,edf->smef", arrived, w_gate, preferred_element_type=jnp.float32)
     up_act = jnp.einsum("smed,edf->smef", arrived, w_up, preferred_element_type=jnp.float32)
     hidden = (jax.nn.silu(gate_act) * up_act).astype(jnp.bfloat16)
-    returned = lax.all_to_all(
-        jnp.einsum("smef,efd->smed", hidden, w_down, preferred_element_type=jnp.float32).astype(
-            jnp.bfloat16
-        ),
-        "expert",
-        split_axis=0,
-        concat_axis=0,
-        tiled=True,
+    value = jnp.einsum("smef,efd->smed", hidden, w_down, preferred_element_type=jnp.float32).astype(
+        jnp.bfloat16
     )
+    ways, here = (lax.axis_size("expert"), lax.axis_index("expert"))
+    width = value.shape[0] // ways
+    turned = jnp.roll(value, -here * width, axis=0)
+    got = [lax.slice_in_dim(turned, 0, width, axis=0)]
+    for far in range(1, ways):
+        sent = lax.slice_in_dim(turned, far * width, (far + 1) * width, axis=0)
+        got.append(lax.ppermute(sent, "expert", [(d, (d + far) % ways) for d in range(ways)]))
+    line = jnp.concatenate(got[::-1], axis=0)
+    returned = jnp.roll(line, (here + 1) * got[0].shape[0], axis=0)
     returned = returned.reshape(num_experts * cap_rows, normed.shape[1])
     gathered = returned[dest_index].reshape(tok_rows, top_count, normed.shape[1])
     combined = jnp.sum(gathered.astype(jnp.float32) * route_w[:, :, None], axis=1).astype(

time: 354 us -> 399 us (1.13)
  the two profiles are of different devices: /device:TPU:15 before, /device:TPU:0 now
where the time goes in v1:
time: 399 us
  waiting for transfers between devices  218 us (55%)
  starting transfers between devices  95.8 us (24%)
  local copies, waits for them, and re-layouts  32.2 us (8%)
  matrix products  27.6 us (7%)
  other arithmetic  25.1 us (6%)
    all_to_all x1, waiting for transfers between devices, local(): lax.all_to_all(outgoing, 'expert', split_axis=0, concat_axis=0, tiled=True)  113 us
    ppermute x15, waiting for transfers between devices, local(): lax.ppermute(sent, 'expert', [(d, (d + far) % ways) for d in range(ways)])  105 us
    ppermute x15, starting transfers between devices, local(): lax.ppermute(sent, 'expert', [(d, (d + far) % ways) for d in range(ways)])  88.2 us
    dot_general x1, matrix products, local(): jnp.einsum('smef,efd->smed', hidden, w_down, preferred_element_type=jnp.f...  16.9 us
    gather x1, local copies, waits for them, and re-layouts, local(): returned[dest_index].reshape(tok_rows, top_count, normed.shape[1])  12.5 us
    scatter x1, local copies, waits for them, and re-layouts, local(): outgoing = jnp.zeros((num_experts * cap_rows, normed.shape[1]), jnp.bfloa...  10.7 us
    dot_general x1, matrix products, local(): jnp.einsum('smed,edf->smef', arrived, w_up, preferred_element_type=jnp.fl...  9.46 us
  transfers between devices with their start and end apart: 16, of which 10 were waited for; matrix products, arithmetic and copies ran while one was open for 1% of the time, Pallas kernels for 0%

profile of v1, /device:TPU:0, one launch (start us, length us, event | category | flops | bytes accessed | tf_op | source)
XLA Modules:
  0.0 398.7 jit_solution(12002354114780307763)
XLA Ops:
  3.4 4.5 %reduce-window.6 = s32[16,8,128]{2,1,0:T(8,128)S(1)} reduce-window(s32[16,8,128]{2,1,0:T(8,128)S(1)} %fusion.37, s32[]{:T(128)} %constant.60.clone.1), window={size=1x1x128 pad=0_0x0_0x127_0}, to_apply=%region_0.0 | reduce-window | flops 2080768 | bytes 131076 | tf_op jit(solution)/shard_map/reduce-window
  10.4 10.7 %scatter_custom_fusion = bf16[1536,2048]{1,0:T(8,128)(2,1)} fusion(s32[1024]{0:T(1024)S(1)} %bitcast.107, bf16[]{:T(256)} %constant.58.clone.1, bf16[128,2048]{1,0:T(8,128)(2,1)} %fusion.33), kind=kCustom, calls=%fused_computation.22 | custom fusion | bytes 6815746 | tf_op jit(solution)/shard_map/scatter | solution.py:34
  21.1 7.6 %all-to-all-start = ((bf16[16,96,1,2048]{3,1,2,0:T(8,128)(2,1)}), bf16[16,96,1,2048]{3,1,2,0:T(8,128)(2,1)}, u32[]{:S(2)}, u32[]{:S(2)}) async-start(bf16[16,96,1,2048]{3,1,2,0:T(8,128)(2,1)} %bitcast.103), calls=%async_computation | async-start | bytes 12582912 | tf_op jit(solution)/shard_map/all_to_all | solution.py:37
  30.0 112.8 %all-to-all-done = bf16[16,96,1,2048]{3,1,2,0:T(8,128)(2,1)} async-done(((bf16[16,96,1,2048]{3,1,2,0:T(8,128)(2,1)}), bf16[16,96,1,2048]{3,1,2,0:T(8,128)(2,1)}, u32[]{:S(2)}, u32[]{:S(2)}) %all-to-all-start) | async-done | bytes 6291488 | tf_op jit(solution)/shard_map/all_to_all | solution.py:37
  142.8 9.5 %fusion.3 = f32[16,96,768]{2,1,0:T(8,128)} fusion(bf16[16,96,1,2048]{3,1,2,0:T(8,128)(2,1)} %all-to-all-done, bf16[1,2048,768]{2,1,0:T(8,128)(2,1)} %param.14), kind=kOutput, calls=%fused_computation.10 | convolution fusion | flops 4831838208 | bytes 14155776 | tf_op jit(solution)/shard_map/smed,edf->smef/dot_general | solution.py:39
  152.3 16.9 %convert_bitcast_fusion = bf16[16,96,1,2048]{3,1,0,2:T(8,128)(2,1)} fusion(bf16[1,768,2048]{2,1,0:T(8,128)(2,1)S(1)} %copy-done, f32[16,96,768]{2,1,0:T(8,128)} %fusion.3, bf16[1,2048,768]{2,1,0:T(8,128)(2,1)} %param.13, bf16[16,96,1,2048]{3,1,2,0:T(8,128)(2,1)} %all-to-all-done), kind=kOutput, calls=%fused_computation.14 | convolution fusion | flops 9673900032 | bytes 23592960 | tf_op jit(solution)/shard_map/smef,efd->smed/dot_general | solution.py:41
  169.2 4.7 %fusion.2 = bf16[16,96,1,2048]{3,1,0,2:T(8,128)(2,1)S(1)} fusion(s32[]{:T(128)S(6)} %select_n.37, bf16[16,96,1,2048]{3,1,0,2:T(8,128)(2,1)} %convert_bitcast_fusion), kind=kLoop, calls=%fused_computation.9 | loop fusion | flops 3145728 | bytes 12582916 | tf_op jit(solution)/shard_map/jit(_roll_dynamic)/concatenate | solution.py:46
  173.9 2.6 copy-done.2
  178.2 26.6 %collective-permute-start = (bf16[1,96,1,2048]{3,1,0,2:T(8,128)(2,1)}, bf16[1,96,1,2048]{3,1,0,2:T(8,128)(2,1)}, u32[]{:S(2)}, u32[]{:S(2)}) collective-permute-start(bf16[1,96,1,2048]{3,1,0,2:T(8,128)(2,1)} %get-tuple-element.22), channel_id=1, source_target_pairs={{0,15},{1,0},{2,1},{3,2},{4,3},{5,4},{6,5},{7,6},{8,7},{9,8},{10,9... | collective-permute-start | bytes 1179656 | tf_op jit(solution)/shard_map/ppermute | solution.py:50
  207.6 6.7 %collective-permute-done = bf16[1,96,1,2048]{3,1,0,2:T(8,128)(2,1)} collective-permute-done((bf16[1,96,1,2048]{3,1,0,2:T(8,128)(2,1)}, bf16[1,96,1,2048]{3,1,0,2:T(8,128)(2,1)}, u32[]{:S(2)}, u32[]{:S(2)}) %collective-permute-start) | collective-permute-done | bytes 393248 | tf_op jit(solution)/shard_map/ppermute | solution.py:50
  214.4 17.1 %collective-permute-start.2 = (bf16[1,96,1,2048]{3,1,0,2:T(8,128)(2,1)}, bf16[1,96,1,2048]{3,1,0,2:T(8,128)(2,1)S(1)}, u32[]{:S(2)}, u32[]{:S(2)}) collective-permute-start(bf16[1,96,1,2048]{3,1,0,2:T(8,128)(2,1)} %get-tuple-element.20), channel_id=1, source_target_pairs={{0,13},{1,14},{2,15},{3,0},{4,1},{5,2},{6,3},{7,4},{8,5},{9,6},{10... | collective-permute-start | bytes 1179656 | tf_op jit(solution)/shard_map/ppermute | solution.py:50
  232.5 7.9 %collective-permute-start.3 = (bf16[1,96,1,2048]{3,1,0,2:T(8,128)(2,1)}, bf16[1,96,1,2048]{3,1,0,2:T(8,128)(2,1)S(1)}, u32[]{:S(2)}, u32[]{:S(2)}) collective-permute-start(bf16[1,96,1,2048]{3,1,0,2:T(8,128)(2,1)} %get-tuple-element.19), channel_id=1, source_target_pairs={{0,12},{1,13},{2,14},{3,15},{4,0},{5,1},{6,2},{7,3},{8,4},{9,5},{1... | collective-permute-start | bytes 1179656 | tf_op jit(solution)/shard_map/ppermute | solution.py:50
  241.3 9.0 %collective-permute-done.3 = bf16[1,96,1,2048]{3,1,0,2:T(8,128)(2,1)S(1)} collective-permute-done((bf16[1,96,1,2048]{3,1,0,2:T(8,128)(2,1)}, bf16[1,96,1,2048]{3,1,0,2:T(8,128)(2,1)S(1)}, u32[]{:S(2)}, u32[]{:S(2)}) %collective-permute-start.3) | collective-permute-done | bytes 393248 | tf_op jit(solution)/shard_map/ppermute | solution.py:50
  250.3 8.4 %collective-permute-done.4 = bf16[1,96,1,2048]{3,1,0,2:T(8,128)(2,1)S(1)} collective-permute-done((bf16[1,96,1,2048]{3,1,0,2:T(8,128)(2,1)}, bf16[1,96,1,2048]{3,1,0,2:T(8,128)(2,1)S(1)}, u32[]{:S(2)}, u32[]{:S(2)}) %collective-permute-start.4) | collective-permute-done | bytes 393248 | tf_op jit(solution)/shard_map/ppermute | solution.py:50
  258.7 18.6 %collective-permute-start.6 = (bf16[1,96,1,2048]{3,1,0,2:T(8,128)(2,1)S(1)}, bf16[1,96,1,2048]{3,1,0,2:T(8,128)(2,1)S(1)}, u32[]{:S(2)}, u32[]{:S(2)}) collective-permute-start(bf16[1,96,1,2048]{3,1,0,2:T(8,128)(2,1)S(1)} %get-tuple-element.16), channel_id=1, source_target_pairs={{0,9},{1,10},{2,11},{3,12},{4,13},{5,14},{6,15},{7,0},{8,1},{9,2},... | collective-permute-start | bytes 1179656 | tf_op jit(solution)/shard_map/ppermute | solution.py:50
  277.4 15.9 %collective-permute-start.7 = (bf16[1,96,1,2048]{3,1,0,2:T(8,128)(2,1)S(1)}, bf16[1,96,1,2048]{3,1,0,2:T(8,128)(2,1)S(1)}, u32[]{:S(2)}, u32[]{:S(2)}) collective-permute-start(bf16[1,96,1,2048]{3,1,0,2:T(8,128)(2,1)S(1)} %get-tuple-element.15), channel_id=1, source_target_pairs={{0,8},{1,9},{2,10},{3,11},{4,12},{5,13},{6,14},{7,15},{8,0},{9,1},... | collective-permute-start | bytes 1179656 | tf_op jit(solution)/shard_map/ppermute | solution.py:50
  293.4 38.1 %collective-permute-done.7 = bf16[1,96,1,2048]{3,1,0,2:T(8,128)(2,1)S(1)} collective-permute-done((bf16[1,96,1,2048]{3,1,0,2:T(8,128)(2,1)S(1)}, bf16[1,96,1,2048]{3,1,0,2:T(8,128)(2,1)S(1)}, u32[]{:S(2)}, u32[]{:S(2)}) %collective-permute-start.7) | collective-permute-done | bytes 393248 | tf_op jit(solution)/shard_map/ppermute | solution.py:50
  331.6 2.7 collective-permute-done.8
  334.3 26.4 %collective-permute-done.9 = bf16[1,96,1,2048]{3,1,0,2:T(8,128)(2,1)S(1)} collective-permute-done((bf16[1,96,1,2048]{3,1,0,2:T(8,128)(2,1)S(1)}, bf16[1,96,1,2048]{3,1,0,2:T(8,128)(2,1)S(1)}, u32[]{:S(2)}, u32[]{:S(2)}) %collective-permute-start.9) | collective-permute-done | bytes 393248 | tf_op jit(solution)/shard_map/ppermute | solution.py:50
  360.7 4.1 %collective-permute-done.10 = bf16[1,96,1,2048]{3,1,0,2:T(8,128)(2,1)S(1)} collective-permute-done((bf16[1,96,1,2048]{3,1,0,2:T(8,128)(2,1)S(1)}, bf16[1,96,1,2048]{3,1,0,2:T(8,128)(2,1)S(1)}, u32[]{:S(2)}, u32[]{:S(2)}) %collective-permute-start.10) | collective-permute-done | bytes 393248 | tf_op jit(solution)/shard_map/ppermute | solution.py:50
  364.8 8.6 %collective-permute-done.11 = bf16[1,96,1,2048]{3,1,0,2:T(8,128)(2,1)S(1)} collective-permute-done((bf16[1,96,1,2048]{3,1,0,2:T(8,128)(2,1)S(1)}, bf16[1,96,1,2048]{3,1,0,2:T(8,128)(2,1)S(1)}, u32[]{:S(2)}, u32[]{:S(2)}) %collective-permute-start.11) | collective-permute-done | bytes 393248 | tf_op jit(solution)/shard_map/ppermute | solution.py:50
  374.6 4.2 %fusion.1 = bf16[16,96,1,2048]{3,1,0,2:T(8,128)(2,1)} fusion(s32[]{:T(128)S(6)} %select_n.39, bf16[16,96,1,2048]{3,1,0,2:T(8,128)(2,1)S(1)} %slice_dynamic-update-slice_fusion), kind=kLoop, calls=%fused_computation.8 | loop fusion | flops 3145728 | bytes 12582916 | tf_op jit(solution)/shard_map/jit(_roll_dynamic)/concatenate | solution.py:52
  378.8 12.5 %gather_fusion = bf16[1024,2048]{1,0:T(8,128)(2,1)} fusion(bf16[1536,2048]{1,0:T(8,128)(2,1)} %bitcast.102, s32[1024]{0:T(1024)S(1)} %broadcast_clamp_fusion), kind=kCustom, calls=%fused_computation | custom fusion | bytes 8392704 | tf_op jit(solution)/shard_map/gather | solution.py:54
  391.4 7.3 %fusion = bf16[128,2048]{1,0:T(8,128)(2,1)} fusion(bf16[1024,2048]{1,0:T(8,128)(2,1)} %gather_fusion, f32[128,8]{1,0:T(8,128)S(1)} %copy-done.3), kind=kLoop, calls=%fused_computation.7 | loop fusion | flops 6029312 | bytes 4722688 | tf_op jit(solution)/shard_map/reduce_sum | solution.py:55
  (68 shorter events, 15.0 us)
Async XLA Ops:
  0.0 152.3 %copy-start = (bf16[1,768,2048]{2,1,0:T(8,128)(2,1)S(1)}, bf16[1,768,2048]{2,1,0:T(8,128)(2,1)}, u32[]{:S(2)}) copy-start(bf16[1,768,2048]{2,1,0:T(8,128)(2,1)} %param.15) | copy-start | bytes 9437188
  21.1 7.6 %copy-start.4 = (bf16[2048,16]{0,1:T(8,128)(2,1)S(1)}, bf16[2048,16]{0,1:T(8,128)(2,1)}, u32[]{:S(2)}) copy-start(bf16[2048,16]{0,1:T(8,128)(2,1)} %param.11) | copy-start | bytes 196612
  21.1 8.9 %copy-start.5 = (s32[128,8]{0,1:T(8,128)S(1)}, s32[128,8]{0,1:T(8,128)}, u32[]{:S(2)}) copy-start(s32[128,8]{0,1:T(8,128)} %param.12) | copy-start | bytes 12292
  21.1 121.8 %all-to-all-start = ((bf16[16,96,1,2048]{3,1,2,0:T(8,128)(2,1)}), bf16[16,96,1,2048]{3,1,2,0:T(8,128)(2,1)}, u32[]{:S(2)}, u32[]{:S(2)}) async-start(bf16[16,96,1,2048]{3,1,2,0:T(8,128)(2,1)} %bitcast.103), calls=%async_computation | async-start | bytes 12582912 | tf_op jit(solution)/shard_map/all_to_all | solution.py:37
  173.9 2.6 copy-start.2
  178.2 36.2 %collective-permute-start = (bf16[1,96,1,2048]{3,1,0,2:T(8,128)(2,1)}, bf16[1,96,1,2048]{3,1,0,2:T(8,128)(2,1)}, u32[]{:S(2)}, u32[]{:S(2)}) collective-permute-start(bf16[1,96,1,2048]{3,1,0,2:T(8,128)(2,1)} %get-tuple-element.22), channel_id=1, source_target_pairs={{0,15},{1,0},{2,1},{3,2},{4,3},{5,4},{6,5},{7,6},{8,7},{9,8},{10,9... | collective-permute-start | bytes 1179656 | tf_op jit(solution)/shard_map/ppermute | solution.py:50
  205.6 26.9 %collective-permute-start.1 = (bf16[1,96,1,2048]{3,1,0,2:T(8,128)(2,1)}, bf16[1,96,1,2048]{3,1,0,2:T(8,128)(2,1)S(1)}, u32[]{:S(2)}, u32[]{:S(2)}) collective-permute-start(bf16[1,96,1,2048]{3,1,0,2:T(8,128)(2,1)} %get-tuple-element.21), channel_id=1, source_target_pairs={{0,14},{1,15},{2,0},{3,1},{4,2},{5,3},{6,4},{7,5},{8,6},{9,7},{10,... | collective-permute-start | bytes 1179656 | tf_op jit(solution)/shard_map/ppermute | solution.py:50
  205.6 167.9 %collective-permute-start.14 = (bf16[1,96,1,2048]{3,1,0,2:T(8,128)(2,1)S(1)}, bf16[1,96,1,2048]{3,1,0,2:T(8,128)(2,1)S(1)}, u32[]{:S(2)}, u32[]{:S(2)}) collective-permute-start(bf16[1,96,1,2048]{3,1,0,2:T(8,128)(2,1)S(1)} %get-tuple-element.8), channel_id=1, source_target_pairs={{0,1},{1,2},{2,3},{3,4},{4,5},{5,6},{6,7},{7,8},{8,9},{9,10},{10,1... | collective-permute-start | bytes 1179656 | tf_op jit(solution)/shard_map/ppermute | solution.py:50
  205.9 167.6 %collective-permute-start.13 = (bf16[1,96,1,2048]{3,1,0,2:T(8,128)(2,1)S(1)}, bf16[1,96,1,2048]{3,1,0,2:T(8,128)(2,1)S(1)}, u32[]{:S(2)}, u32[]{:S(2)}) collective-permute-start(bf16[1,96,1,2048]{3,1,0,2:T(8,128)(2,1)S(1)} %get-tuple-element.9), channel_id=1, source_target_pairs={{0,2},{1,3},{2,4},{3,5},{4,6},{5,7},{6,8},{7,9},{8,10},{9,11},{10,... | collective-permute-start | bytes 1179656 | tf_op jit(solution)/shard_map/ppermute | solution.py:50
  207.6 165.8 %collective-permute-start.12 = (bf16[1,96,1,2048]{3,1,0,2:T(8,128)(2,1)S(1)}, bf16[1,96,1,2048]{3,1,0,2:T(8,128)(2,1)S(1)}, u32[]{:S(2)}, u32[]{:S(2)}) collective-permute-start(bf16[1,96,1,2048]{3,1,0,2:T(8,128)(2,1)S(1)} %get-tuple-element.10), channel_id=1, source_target_pairs={{0,3},{1,4},{2,5},{3,6},{4,7},{5,8},{6,9},{7,10},{8,11},{9,12},{10... | collective-permute-start | bytes 1179656 | tf_op jit(solution)/shard_map/ppermute | solution.py:50
  214.4 26.9 %collective-permute-start.2 = (bf16[1,96,1,2048]{3,1,0,2:T(8,128)(2,1)}, bf16[1,96,1,2048]{3,1,0,2:T(8,128)(2,1)S(1)}, u32[]{:S(2)}, u32[]{:S(2)}) collective-permute-start(bf16[1,96,1,2048]{3,1,0,2:T(8,128)(2,1)} %get-tuple-element.20), channel_id=1, source_target_pairs={{0,13},{1,14},{2,15},{3,0},{4,1},{5,2},{6,3},{7,4},{8,5},{9,6},{10... | collective-permute-start | bytes 1179656 | tf_op jit(solution)/shard_map/ppermute | solution.py:50
  232.5 17.8 %collective-permute-start.3 = (bf16[1,96,1,2048]{3,1,0,2:T(8,128)(2,1)}, bf16[1,96,1,2048]{3,1,0,2:T(8,128)(2,1)S(1)}, u32[]{:S(2)}, u32[]{:S(2)}) collective-permute-start(bf16[1,96,1,2048]{3,1,0,2:T(8,128)(2,1)} %get-tuple-element.19), channel_id=1, source_target_pairs={{0,12},{1,13},{2,14},{3,15},{4,0},{5,1},{6,2},{7,3},{8,4},{9,5},{1... | collective-permute-start | bytes 1179656 | tf_op jit(solution)/shard_map/ppermute | solution.py:50
  241.3 17.4 %collective-permute-start.4 = (bf16[1,96,1,2048]{3,1,0,2:T(8,128)(2,1)}, bf16[1,96,1,2048]{3,1,0,2:T(8,128)(2,1)S(1)}, u32[]{:S(2)}, u32[]{:S(2)}) collective-permute-start(bf16[1,96,1,2048]{3,1,0,2:T(8,128)(2,1)} %get-tuple-element.18), channel_id=1, source_target_pairs={{0,11},{1,12},{2,13},{3,14},{4,15},{5,0},{6,1},{7,2},{8,3},{9,4},{... | collective-permute-start | bytes 1179656 | tf_op jit(solution)/shard_map/ppermute | solution.py:50
  250.3 27.0 %collective-permute-start.5 = (bf16[1,96,1,2048]{3,1,0,2:T(8,128)(2,1)}, bf16[1,96,1,2048]{3,1,0,2:T(8,128)(2,1)S(1)}, u32[]{:S(2)}, u32[]{:S(2)}) collective-permute-start(bf16[1,96,1,2048]{3,1,0,2:T(8,128)(2,1)} %get-tuple-element.17), channel_id=1, source_target_pairs={{0,10},{1,11},{2,12},{3,13},{4,14},{5,15},{6,0},{7,1},{8,2},{9,3},... | collective-permute-start | bytes 1179656 | tf_op jit(solution)/shard_map/ppermute | solution.py:50
  258.7 34.6 %collective-permute-start.6 = (bf16[1,96,1,2048]{3,1,0,2:T(8,128)(2,1)S(1)}, bf16[1,96,1,2048]{3,1,0,2:T(8,128)(2,1)S(1)}, u32[]{:S(2)}, u32[]{:S(2)}) collective-permute-start(bf16[1,96,1,2048]{3,1,0,2:T(8,128)(2,1)S(1)} %get-tuple-element.16), channel_id=1, source_target_pairs={{0,9},{1,10},{2,11},{3,12},{4,13},{5,14},{6,15},{7,0},{8,1},{9,2},... | collective-permute-start | bytes 1179656 | tf_op jit(solution)/shard_map/ppermute | solution.py:50
  277.4 54.2 %collective-permute-start.7 = (bf16[1,96,1,2048]{3,1,0,2:T(8,128)(2,1)S(1)}, bf16[1,96,1,2048]{3,1,0,2:T(8,128)(2,1)S(1)}, u32[]{:S(2)}, u32[]{:S(2)}) collective-permute-start(bf16[1,96,1,2048]{3,1,0,2:T(8,128)(2,1)S(1)} %get-tuple-element.15), channel_id=1, source_target_pairs={{0,8},{1,9},{2,10},{3,11},{4,12},{5,13},{6,14},{7,15},{8,0},{9,1},... | collective-permute-start | bytes 1179656 | tf_op jit(solution)/shard_map/ppermute | solution.py:50
  293.3 40.9 %collective-permute-start.8 = (bf16[1,96,1,2048]{3,1,0,2:T(8,128)(2,1)S(1)}, bf16[1,96,1,2048]{3,1,0,2:T(8,128)(2,1)S(1)}, u32[]{:S(2)}, u32[]{:S(2)}) collective-permute-start(bf16[1,96,1,2048]{3,1,0,2:T(8,128)(2,1)S(1)} %get-tuple-element.14), channel_id=1, source_target_pairs={{0,7},{1,8},{2,9},{3,10},{4,11},{5,12},{6,13},{7,14},{8,15},{9,0},... | collective-permute-start | bytes 1179656 | tf_op jit(solution)/shard_map/ppermute | solution.py:50
  331.5 29.1 %collective-permute-start.9 = (bf16[1,96,1,2048]{3,1,0,2:T(8,128)(2,1)S(1)}, bf16[1,96,1,2048]{3,1,0,2:T(8,128)(2,1)S(1)}, u32[]{:S(2)}, u32[]{:S(2)}) collective-permute-start(bf16[1,96,1,2048]{3,1,0,2:T(8,128)(2,1)S(1)} %get-tuple-element.13), channel_id=1, source_target_pairs={{0,6},{1,7},{2,8},{3,9},{4,10},{5,11},{6,12},{7,13},{8,14},{9,15},... | collective-permute-start | bytes 1179656 | tf_op jit(solution)/shard_map/ppermute | solution.py:50
  334.2 30.6 %collective-permute-start.10 = (bf16[1,96,1,2048]{3,1,0,2:T(8,128)(2,1)S(1)}, bf16[1,96,1,2048]{3,1,0,2:T(8,128)(2,1)S(1)}, u32[]{:S(2)}, u32[]{:S(2)}) collective-permute-start(bf16[1,96,1,2048]{3,1,0,2:T(8,128)(2,1)S(1)} %get-tuple-element.12), channel_id=1, source_target_pairs={{0,5},{1,6},{2,7},{3,8},{4,9},{5,10},{6,11},{7,12},{8,13},{9,14},{... | collective-permute-start | bytes 1179656 | tf_op jit(solution)/shard_map/ppermute | solution.py:50
  360.7 12.7 %collective-permute-start.11 = (bf16[1,96,1,2048]{3,1,0,2:T(8,128)(2,1)S(1)}, bf16[1,96,1,2048]{3,1,0,2:T(8,128)(2,1)S(1)}, u32[]{:S(2)}, u32[]{:S(2)}) collective-permute-start(bf16[1,96,1,2048]{3,1,0,2:T(8,128)(2,1)S(1)} %get-tuple-element.11), channel_id=1, source_target_pairs={{0,4},{1,5},{2,6},{3,7},{4,8},{5,9},{6,10},{7,11},{8,12},{9,13},{1... | collective-permute-start | bytes 1179656 | tf_op jit(solution)/shard_map/ppermute | solution.py:50
  378.8 12.5 %copy-start.3 = (f32[128,8]{1,0:T(8,128)S(1)}, f32[128,8]{1,0:T(8,128)}, u32[]{:S(2)}) copy-start(f32[128,8]{1,0:T(8,128)} %copy.31) | copy-start | bytes 12292
  378.8 19.9 %copy-start.1 = (bf16[1,768,2048]{2,1,0:T(8,128)(2,1)S(1)}, bf16[1,768,2048]{2,1,0:T(8,128)(2,1)}, u32[]{:S(2)}) copy-start(bf16[1,768,2048]{2,1,0:T(8,128)(2,1)} %param.15) | copy-start | bytes 9437188
